TPU v7x, 32 devices: a whole 2x2x4 slice. The times are simulated.
32 devices in a mesh: facet: 4 (over z), col: 8 (over y, x, core).
Axes of the slice: x: 2, y: 2, z: 4, core: 2. Of those that a mesh axis runs over, the one named last changes fastest.
Arguments:
- sky_re: bfloat16 [4, 4096, 4096], P('facet', None, 'col'), may hold values from -6 to 6
- sky_im: bfloat16 [4, 4096, 4096], P('facet', None, 'col'), may hold values from -6 to 6
- col_offsets: int32 [2], replicated, may hold values from 0 to 65280
- sub_offsets: int32 [4], replicated, may hold values from 0 to 65280
- kernel: float32 [16, 8], replicated, may hold values from 0.05 to 1
- vis_count: int32 [4, 32], P('facet', 'col'), may hold values from 0 to 128, as said below
- cell_index: int32 [2, 4, 32, 128], P(None, 'facet', 'col'), may hold values from 0 to 248
- frac_index: int32 [2, 4, 32, 128], P(None, 'facet', 'col'), may hold values from 0 to 15
Outputs:
- vis_re: float32 [4, 32, 128], P('facet', 'col')
- vis_im: float32 [4, 32, 128], P('facet', 'col')
Inputs may be any that keep to these rules, and one draw needn't show every extreme that they name: Within each subgrid the blocks with visibilities come first and block 0 holds 128; in some subgrid all 32 blocks hold visibilities; a block's visibilities fill its first vis_count slots.
All inputs are finite; a program needn't handle non-finite values.
Results may differ from a plain program's by a relative error of at most 0.0037.
Values may be sent and summed in bfloat16 or wider, within the bound.
A program may use at most 64 MiB of HBM per device.

v0:
```python
import math

import jax
import jax.numpy as jnp
from jax import lax
from jax.sharding import PartitionSpec as P

N_IMG = 65536
S = 256
SCOL = 2


def modular_product(left_ints, right_ints):
    upper_part = right_ints // 256
    lower_part = right_ints % 256
    product = left_ints[:, None] * upper_part[None, :] % N_IMG
    product = product * 256 % N_IMG
    return (product + left_ints[:, None] * lower_part[None, :]) % N_IMG


def cos_sin(left_ints, right_ints, factor):
    angles = modular_product(left_ints, right_ints).astype(jnp.float32) * (2.0 * math.pi / N_IMG)
    return (jnp.cos(angles) * factor, jnp.sin(angles) * factor)


def first_axis(facet_image, table, local_cols):
    product = jnp.dot(table, facet_image, preferred_element_type=jnp.float32)
    real_part = product[:S, :local_cols] + product[S:, local_cols:]
    imag_part = product[:S, local_cols:] - product[S:, :local_cols]
    return jnp.stack([real_part, imag_part]).astype(jnp.bfloat16)


def second_axis(band_rows, starts, anchor, second_table):
    mod_cos, mod_sin = cos_sin(starts, anchor, 1.0)
    shifted_re = band_rows[0][None] * mod_cos[:, None] + band_rows[1][None] * mod_sin[:, None]
    shifted_im = band_rows[1][None] * mod_cos[:, None] - band_rows[0][None] * mod_sin[:, None]
    stacked = jnp.concatenate([shifted_re, shifted_im], axis=0).astype(jnp.bfloat16)
    per_column = starts.shape[0]
    row_count = band_rows.shape[1]
    product = jnp.dot(
        stacked.reshape(2 * per_column * row_count, -1),
        second_table,
        preferred_element_type=jnp.float32,
    )
    product = product.reshape(2, per_column, row_count, 2 * S)
    term_re = product[0, :, :, :S] + product[1, :, :, S:]
    term_im = product[1, :, :, :S] - product[0, :, :, S:]
    return jnp.concatenate([term_re, term_im], axis=2)


def lookup(frac_ints, kernel):
    table_rows = jnp.arange(kernel.shape[0], dtype=jnp.int32)
    matches = frac_ints[..., None] == table_rows
    return jnp.sum(jnp.where(matches[..., None], kernel, 0.0), axis=-2)


def spread(cell_ints, tap_values):
    columns = jnp.arange(S, dtype=jnp.int32)
    summed = jnp.zeros(cell_ints.shape + (S,), jnp.float32)
    for offset in range(tap_values.shape[-1]):
        summed = summed + jnp.where(
            columns == cell_ints[..., None] + offset, tap_values[..., offset : offset + 1], 0.0
        )
    return summed


def visibilities(row_sum, col_weights, in_block):
    vis_real = jnp.where(in_block, jnp.sum(row_sum[..., :S] * col_weights, axis=-1), 0.0)
    vis_imag = jnp.where(in_block, jnp.sum(row_sum[..., S:] * col_weights, axis=-1), 0.0)
    return (vis_real, vis_imag)


def facet_table(facet_anchor, spectral, pixels, facets):
    cos_tab, sin_tab = cos_sin(facet_anchor, spectral, 1.0 / math.sqrt(pixels * facets))
    return jnp.concatenate([cos_tab, sin_tab], axis=1).astype(jnp.bfloat16)


def local(sky_re, sky_im, col_offsets, sub_offsets, kernel, vis_count, cell_index, frac_index):
    pixels = sky_re.shape[1]
    local_cols = sky_re.shape[2]
    facets = lax.axis_size("facet")
    per_column = sub_offsets.shape[0] // SCOL
    owned = vis_count.shape[0]
    facet_image = jnp.concatenate([sky_re[0], sky_im[0]], axis=1)
    spatial = jnp.arange(pixels, dtype=jnp.int32)
    spectral = jnp.arange(S, dtype=jnp.int32)

    def column_table(column):
        cos_part, sin_part = cos_sin(
            col_offsets[column] + spectral, spatial, 1.0 / math.sqrt(pixels)
        )
        return jnp.concatenate([cos_part, sin_part], axis=0).astype(jnp.bfloat16)

    def column_starts(column):
        return sub_offsets[column * per_column : (column + 1) * per_column]

    pieces = jnp.stack(
        [first_axis(facet_image, column_table(column), local_cols) for column in range(SCOL)]
    )
    received = lax.all_to_all(pieces, "col", split_axis=2, concat_axis=3, tiled=True)
    column_bands = [received[column] for column in range(SCOL)]
    anchor = lax.axis_index("facet") * pixels + spatial
    second_table = facet_table(anchor, spectral, pixels, facets)
    column_terms = [
        second_axis(column_bands[column], column_starts(column), anchor, second_table)
        for column in range(SCOL)
    ]
    partial_value = jnp.concatenate(column_terms, axis=0)
    grid_rows = lax.psum_scatter(partial_value, "facet", scatter_dimension=0, tiled=True).astype(
        jnp.bfloat16
    )
    blocks = vis_count.shape[1]
    block_slots = cell_index.shape[-1]
    slot_ids = jnp.arange(block_slots, dtype=jnp.int32)
    row_weights = spread(cell_index[0], lookup(frac_index[0], kernel)).astype(jnp.bfloat16)
    row_weights = row_weights.reshape(owned, blocks * block_slots, S)
    col_weights = spread(cell_index[1], lookup(frac_index[1], kernel)).reshape(
        owned, blocks * block_slots, S
    )
    row_sum = jnp.einsum(
        "svr,src->svc",
        row_weights,
        lax.all_gather(grid_rows, "col", axis=1, tiled=True),
        preferred_element_type=jnp.float32,
    )
    in_block = (slot_ids < vis_count[..., None]).reshape(owned, blocks * block_slots)
    flat_re, flat_im = visibilities(row_sum, col_weights, in_block)
    vis_real = flat_re.reshape(owned, blocks, block_slots)
    vis_imag = flat_im.reshape(owned, blocks, block_slots)
    return (vis_real, vis_imag)


def solution(mesh):
    placed = (
        P("facet", None, "col"),
        P("facet", None, "col"),
        P(),
        P(),
        P(),
        P("facet", "col"),
        P(None, "facet", "col", None),
        P(None, "facet", "col", None),
    )
    return jax.shard_map(
        local,
        mesh=mesh,
        in_specs=placed,
        out_specs=(P("facet", "col", None), P("facet", "col", None)),
        check_vma=False,
    )
```

profile of v0, /device:TPU:0, one launch (start us, length us, event | category | flops | bytes accessed | tf_op | source)
XLA Modules:
  0.0 139.6 jit_solution(15522688869136861759)
XLA Ops:
  7.2 1.3 fusion.103
  8.5 1.3 iota_add_fusion.1
  9.8 0.0 copy-start.6
  9.8 0.0 copy-start.7
  9.8 40.9 %multiply_convert_fusion.5 = (bf16[256,4096]{1,0:T(8,128)(2,1)S(1)}, bf16[256,4096]{1,0:T(8,128)(2,1)S(1)}, bf16[256,4096]{1,0:T(8,128)(2,1)S(1)}, bf16[256,4096]{1,0:T(8,128)(2,1)S(1)}) fusion(s32[4096]{0:T(1024)S(1)} %get-tuple-element.78, s32[4096]{0:T(1024)S(1)} %get-tuple-element.79, s32[256]{0:T(256)S(1)} %get-tuple-element.81, ...), kind=kLoop, calls=%fused_computation.69 | loop fusion | flops 90177536 | bytes 8423424 | tf_op jit(solution)/shard_map/convert.20
  50.7 0.0 copy-done.6
  50.7 0.0 copy-done.7
  50.7 4.5 %fusion.1 = f32[512,1024]{1,0:T(8,128)S(1)} fusion(bf16[4096,512]{1,0:T(8,128)(2,1)S(1)} %bitcast.141, bf16[4096,512]{1,0:T(8,128)(2,1)S(1)} %bitcast.143, bf16[256,4096]{1,0:T(8,128)(2,1)S(1)} %get-tuple-element.23, bf16[256,4096]{1,0:T(8,128)(2,1)S(1)} %get-tuple-element.22), kind=kOutput, calls=%fused_computation.35 | convolution fusion | flops 4320133120 | bytes 14680064 | tf_op jit(solution)/shard_map/dot_general | solution.py:27
  55.2 0.2 fusion.37
  55.4 4.5 %fusion = f32[512,1024]{1,0:T(8,128)S(1)} fusion(bf16[4096,512]{1,0:T(8,128)(2,1)S(1)} %bitcast.142, bf16[4096,512]{1,0:T(8,128)(2,1)S(1)} %bitcast.144, bf16[256,4096]{1,0:T(8,128)(2,1)S(1)} %get-tuple-element.32, bf16[256,4096]{1,0:T(8,128)(2,1)S(1)} %get-tuple-element.33), kind=kOutput, calls=%fused_computation.34 | convolution fusion | flops 4320133120 | bytes 14680064 | tf_op jit(solution)/shard_map/dot_general | solution.py:27
  59.9 0.0 copy-start.1
  59.9 0.0 copy-start.4
  59.9 0.0 copy-start.3
  59.9 0.2 fusion.39
  60.1 0.1 maximum_maximum_fusion
  60.2 0.0 copy-start.2
  60.2 2.1 %copy.17 = bf16[2,2,256,512]{3,1,0,2:T(2,128)(2,1)} copy(bf16[2,2,256,512]{3,2,1,0:T(8,128)(2,1)S(1)} %maximum_maximum_fusion) | data formatting | bytes 2097152 | tf_op jit(solution)/shard_map/stack | solution.py:97
  62.3 5.2 %all-to-all-start = ((bf16[2,2,256,512]{3,1,0,2:T(2,128)(2,1)}), bf16[2,2,256,512]{3,1,0,2:T(2,128)(2,1)S(1)}, u32[]{:S(2)}, u32[]{:S(2)}) async-start(bf16[2,2,256,512]{3,1,0,2:T(2,128)(2,1)} %copy.17), calls=%async_computation | async-start | bytes 2097152 | tf_op jit(solution)/shard_map/all_to_all | solution.py:100
  67.5 0.0 reduce-scatter.2.cloned.1.call-start
  67.6 0.0 copy-done.1
  67.6 0.0 copy-done.4
  67.6 0.1 fusion.102
  67.7 0.0 copy-done.3
  67.7 23.1 %multiply_convert_fusion.1 = (bf16[4096,256]{1,0:T(8,128)(2,1)S(1)}, bf16[4096,256]{1,0:T(8,128)(2,1)}) fusion(s32[256]{0:T(256)S(1)} %get-tuple-element.82, s32[256]{0:T(256)S(1)} %get-tuple-element.83, s32[4096]{0:T(1024)S(1)} %iota_add_fusion), kind=kLoop, calls=%fused_computation.65 | loop fusion | flops 45088768 | bytes 4212736 | tf_op jit(solution)/shard_map/convert.6
  90.9 0.0 copy-done.2
  90.9 0.1 copy.16
  91.0 1.3 fusion.94
  92.3 0.0 all-to-all-done
  92.3 0.6 copy.25
  92.9 0.0 copy-start
  92.9 0.2 slice_convert_fusion.3
  93.0 0.3 copy.20
  93.4 0.3 copy.21
  93.7 0.2 add_convert_fusion.1
  93.9 0.1 pad_maximum_fusion.3
  94.0 0.4 copy-done
  94.5 0.8 fusion.30
  95.3 0.3 copy.22
  95.6 0.3 copy.23
  95.9 0.3 add_convert_fusion
  96.2 0.1 pad_maximum_fusion.4
  96.3 0.8 fusion.29
  97.1 0.0 copy-start.5
  97.1 0.7 maximum_maximum_fusion.1
  97.8 0.0 reduce-scatter.2.cloned.1.call-update
  97.8 0.1 select_reduce_fusion
  98.0 21.7 %reduce-scatter.2.cloned.1.call-done = f32[1,32,512]{2,1,0:T(8,128)} async-done(((f32[4,32,512]{2,1,0:T(8,128)}), f32[1,32,512]{2,1,0:T(8,128)}) %reduce-scatter.2.cloned.1.call-update) | async-done | bytes 65552 | tf_op jit(solution)/shard_map/reduce_scatter | solution.py:109
  119.7 0.8 convert_element_type.133
  120.5 9.3 %all_gather.3 = bf16[1,256,512]{2,1,0:T(8,128)(2,1)S(1)} all-gather(bf16[1,32,512]{2,1,0:T(8,128)(2,1)S(1)} %convert_element_type.133), channel_id=1, replica_groups=mesh['facet'=4,'col'=8] {'col'}, dimensions={1}, use_global_device_ids=true | all-gather | bytes 294912 | tf_op jit(solution)/shard_map/all_gather | solution.py:123
  129.8 1.8 %convolution_bitcast_fusion = f32[1,512,512]{1,2,0:T(8,128)S(1)} fusion(bf16[1,256,512]{2,1,0:T(8,128)(2,1)S(1)} %all_gather.3, f32[512]{0:T(512)S(1)} %bitcast.133, s32[512]{0:T(512)S(1)} %get-tuple-element.67, f32[512]{0:T(512)S(1)} %bitcast.134, s32[512]{0:T(512)S(1)} %get-tuple-element.66, f32[512]{0:T(512)S(1)} %bitcast.135, ...), kind=kOutput, calls=%fused_computation.72 | convolution fusion | flops 137363456 | bytes 1343488 | tf_op jit(solution)/shard_map/svr,src->svc/dot_general | solution.py:120
  131.6 0.5 fusion.31
  132.1 0.0 copy-done.5
  132.1 0.7 bitcast_select_fusion
  (12 shorter events, 0.1 us)
Async XLA Ops:
  9.8 40.9 %copy-start.6 = (bf16[1,4096,512]{2,1,0:T(8,128)(2,1)S(1)}, bf16[1,4096,512]{2,1,0:T(8,128)(2,1)}, u32[]{:S(2)}) copy-start(bf16[1,4096,512]{2,1,0:T(8,128)(2,1)} %param.9) | copy-start | bytes 12582916
  9.8 40.9 %copy-start.7 = (bf16[1,4096,512]{2,1,0:T(8,128)(2,1)S(1)}, bf16[1,4096,512]{2,1,0:T(8,128)(2,1)}, u32[]{:S(2)}) copy-start(bf16[1,4096,512]{2,1,0:T(8,128)(2,1)} %param.8) | copy-start | bytes 12582916
  59.9 7.6 %copy-start.1 = (s32[2,1,4,128]{3,2,1,0:T(4,128)S(1)}, s32[2,1,4,128]{3,2,1,0:T(4,128)}, u32[]{:S(2)}) copy-start(s32[2,1,4,128]{3,2,1,0:T(4,128)} %param.14) | copy-start | bytes 12292
  59.9 7.7 %copy-start.4 = (s32[4]{0:T(128)S(1)}, s32[4]{0:T(128)}, u32[]{:S(2)}) copy-start(s32[4]{0:T(128)} %param.11) | copy-start | bytes 52
  59.9 7.8 %copy-start.3 = (s32[2,1,4,128]{3,2,1,0:T(4,128)S(1)}, s32[2,1,4,128]{3,2,1,0:T(4,128)}, u32[]{:S(2)}) copy-start(s32[2,1,4,128]{3,2,1,0:T(4,128)} %param.15) | copy-start | bytes 12292
  60.2 30.6 %copy-start.2 = (f32[16,8]{0,1:T(8,128)S(1)}, f32[16,8]{0,1:T(8,128)}, u32[]{:S(2)}) copy-start(f32[16,8]{0,1:T(8,128)} %param.12) | copy-start | bytes 1540
  62.3 30.0 %all-to-all-start = ((bf16[2,2,256,512]{3,1,0,2:T(2,128)(2,1)}), bf16[2,2,256,512]{3,1,0,2:T(2,128)(2,1)S(1)}, u32[]{:S(2)}, u32[]{:S(2)}) async-start(bf16[2,2,256,512]{3,1,0,2:T(2,128)(2,1)} %copy.17), calls=%async_computation | async-start | bytes 2097152 | tf_op jit(solution)/shard_map/all_to_all | solution.py:100
  67.5 52.2 %reduce-scatter.2.cloned.1.call-start = ((), (), s32[]{:S(2)}) async-start(), calls=%async_computation.2 | async-start | bytes 327680 | tf_op jit(solution)/shard_map/reduce_scatter | solution.py:109
  92.9 1.6 %copy-start = (bf16[4096,256]{1,0:T(8,128)(2,1)S(1)}, bf16[4096,256]{1,0:T(8,128)(2,1)}, u32[]{:S(2)}) copy-start(bf16[4096,256]{1,0:T(8,128)(2,1)} %get-tuple-element.35) | copy-start | bytes 6291460
  97.1 35.1 %copy-start.5 = (s32[1,4]{1,0:T(1,128)S(1)}, s32[1,4]{1,0:T(1,128)}, u32[]{:S(2)}) copy-start(s32[1,4]{1,0:T(1,128)} %param.13) | copy-start | bytes 52
Sparse Core Ops, SparseCore 0:
  98.0 21.6 reduce-scatter.1
where the time goes:
time: 140 us
  other arithmetic  70.8 us (51%)
  waiting for transfers between devices  21.7 us (16%)
  between operations  14.4 us (10%)
  matrix products  12.4 us (9%)
  blocking collectives  9.25 us (7%)
  local copies, waits for them, and re-layouts  5.84 us (4%)
  starting transfers between devices  5.24 us (4%)
    another operation x4, other arithmetic  64.5 us
    reduce_scatter x1, waiting for transfers between devices, local(): lax.psum_scatter(partial_value, 'facet', scatter_dimension=0, tiled=True)  21.7 us
    all_gather x1, blocking collectives, local(): lax.all_gather(grid_rows, 'col', axis=1, tiled=True)  9.25 us
    dot_general x2, matrix products, first_axis(): product = jnp.dot(table, facet_image, preferred_element_type=jnp.float32)  9.01 us
    all_to_all x1, starting transfers between devices, local(): lax.all_to_all(pieces, 'col', split_axis=2, concat_axis=3, tiled=True)  5.2 us
  transfers between devices with their start and end apart: 2, of which 1 were waited for; matrix products, arithmetic and copies ran while one was open for 18% of the time, Pallas kernels for 0%

commit v1 on v0

--- a/solution.py
+++ b/solution.py
@@ -23,8 +23,19 @@
     return (jnp.cos(angles) * factor, jnp.sin(angles) * factor)
 
 
+def split_table(left_ints, right_ints, factor):
+    parts = 64
+    coarse_cos, coarse_sin = cos_sin(left_ints[::parts], right_ints, factor)
+    fine_cos, fine_sin = cos_sin(left_ints[:parts] - left_ints[0], right_ints, 1.0)
+    cos_tab = coarse_cos[:, None] * fine_cos[None] - coarse_sin[:, None] * fine_sin[None]
+    sin_tab = coarse_sin[:, None] * fine_cos[None] + coarse_cos[:, None] * fine_sin[None]
+    return (cos_tab.reshape(left_ints.shape[0], -1), sin_tab.reshape(left_ints.shape[0], -1))
+
+
 def first_axis(facet_image, table, local_cols):
-    product = jnp.dot(table, facet_image, preferred_element_type=jnp.float32)
+    product = lax.dot_general(
+        table, facet_image, (((0,), (0,)), ((), ())), preferred_element_type=jnp.float32
+    )
     real_part = product[:S, :local_cols] + product[S:, local_cols:]
     imag_part = product[:S, local_cols:] - product[S:, :local_cols]
     return jnp.stack([real_part, imag_part]).astype(jnp.bfloat16)
@@ -71,7 +82,7 @@
 
 
 def facet_table(facet_anchor, spectral, pixels, facets):
-    cos_tab, sin_tab = cos_sin(facet_anchor, spectral, 1.0 / math.sqrt(pixels * facets))
+    cos_tab, sin_tab = split_table(facet_anchor, spectral, 1.0 / math.sqrt(pixels * facets))
     return jnp.concatenate([cos_tab, sin_tab], axis=1).astype(jnp.bfloat16)
 
 
@@ -86,10 +97,10 @@
     spectral = jnp.arange(S, dtype=jnp.int32)
 
     def column_table(column):
-        cos_part, sin_part = cos_sin(
-            col_offsets[column] + spectral, spatial, 1.0 / math.sqrt(pixels)
+        cos_part, sin_part = split_table(
+            spatial, col_offsets[column] + spectral, 1.0 / math.sqrt(pixels)
         )
-        return jnp.concatenate([cos_part, sin_part], axis=0).astype(jnp.bfloat16)
+        return jnp.concatenate([cos_part, sin_part], axis=1).astype(jnp.bfloat16)
 
     def column_starts(column):
         return sub_offsets[column * per_column : (column + 1) * per_column]

time: 140 us -> 94.8 us (0.68)
  other arithmetic: 70.8 us -> 16 us
  waiting for transfers between devices: 21.7 us -> 28 us
  matrix products: 12.4 us -> 14.6 us
    another operation x4 -> x5, other arithmetic: 64.5 us -> 6.87 us
    all_to_all x1, waiting for transfers between devices: 0.01 us -> 8.56 us  [local(): lax.all_to_all(pieces, 'col', split_axis=2, concat_axis=3, tiled=True)]
    reduce_scatter x1, waiting for transfers between devices: 21.7 us -> 19.4 us  [local(): lax.psum_scatter(partial_value, 'facet', scatter_dimension=0, tiled=True)]
    dot_general x2, matrix products: 9.01 us -> 11.2 us  [first_axis(): lax.dot_general(table, facet_image, (((0,), (0,)), ((), ())), preferred_e...]
    mul x0 -> x2, other arithmetic: none -> 2.03 us  [cos_sin(): return (jnp.cos(angles) * factor, jnp.sin(angles) * factor)]
  transfers between devices with their start and end apart: 2 -> 2, of which waited for: 1 -> 2; matrix products, arithmetic and copies ran while one was open for 18% -> 7% of each run, Pallas kernels for 0% -> 0%
where the time goes in v1:
time: 94.8 us; the launch traced here: 94.4 us
  waiting for transfers between devices  28 us (30%)
  other arithmetic  16 us (17%)
  matrix products  14.6 us (15%)
  between operations  14.4 us (15%)
  blocking collectives  9.25 us (10%)
  local copies, waits for them, and re-layouts  6.81 us (7%)
  starting transfers between devices  5.41 us (6%)
    reduce_scatter x1, waiting for transfers between devices, local(): lax.psum_scatter(partial_value, 'facet', scatter_dimension=0, tiled=True)  19.4 us
    dot_general x2, matrix products, first_axis(): lax.dot_general(table, facet_image, (((0,), (0,)), ((), ())), preferred_e...  11.2 us
    all_gather x1, blocking collectives, local(): lax.all_gather(grid_rows, 'col', axis=1, tiled=True)  9.25 us
    all_to_all x1, waiting for transfers between devices, local(): lax.all_to_all(pieces, 'col', split_axis=2, concat_axis=3, tiled=True)  8.56 us
    another operation x5, other arithmetic  6.87 us
    all_to_all x1, starting transfers between devices, local(): lax.all_to_all(pieces, 'col', split_axis=2, concat_axis=3, tiled=True)  5.2 us
    another operation x1, local copies, waits for them, and re-layouts, local(): jnp.stack([first_axis(facet_image, column_table(column), local_cols) for...  2.06 us
    mul x2, other arithmetic, cos_sin(): return (jnp.cos(angles) * factor, jnp.sin(angles) * factor)  2.03 us
  transfers between devices with their start and end apart: 2, of which 2 were waited for; matrix products, arithmetic and copies ran while one was open for 7% of the time, Pallas kernels for 0%

profile of v1, /device:TPU:0, one launch (start us, length us, event | category | flops | bytes accessed | tf_op | source)
XLA Modules:
  0.0 94.4 jit_solution(9646276468159940444)
XLA Ops:
  7.2 1.3 %fusion.125 = (s32[1]{0:T(128)}, s32[1]{0:T(128)}) fusion(s32[2]{0:T(128)} %param.10), kind=kLoop, calls=%fused_computation.320 | loop fusion | bytes 16 | tf_op jit(solution)/shard_map/slice | solution.py:101
  8.5 0.7 and_select_fusion.10
  9.1 0.7 and_select_fusion.8
  9.8 0.1 slice.197
  10.0 0.0 copy-start.6
  10.0 1.3 %cosine_multiply_fusion.1 = (f32[64,256]{1,0:T(8,128)S(1)}, f32[64,256]{1,0:T(8,128)S(1)}, f32[64,256]{1,0:T(8,128)S(1)}, f32[64,256]{1,0:T(8,128)S(1)}, f32[64,...) fusion(s32[256]{0:T(256)S(1)} %get-tuple-element.98, ...), kind=kLoop, calls=%fused_computation.217 | loop fusion | flops 2621440 | bytes 528896 | tf_op jit(solution)/shard_map/mul | solution.py:23
  11.3 1.7 %subtract_convert_fusion.2 = (bf16[64,64,256]{2,1,0:T(8,128)(2,1)S(1)}, bf16[64,64,256]{2,1,0:T(8,128)(2,1)S(1)}) fusion(f32[64,256]{1,0:T(8,128)S(1)} %get-tuple-element.87, f32[64,256]{1,0:T(8,128)S(1)} %get-tuple-element.88, f32[64,256]{1,0:T(8,128)S(1)} %get-tuple-element.86, f32[64,256]{1,0:T(8,128)S(1)} %get-tuple-element.89), kind=kLoop, calls=%fused_computation.15 | loop fusion | flops 8388608 | bytes 4456448 | tf_op jit(solution)/shard_map/convert.27
  13.0 0.0 copy-done.6
  13.0 6.7 %fusion.1 = f32[512,1024]{1,0:T(8,128)S(1)} fusion(bf16[4096,512]{1,0:T(8,128)(2,1)S(1)} %bitcast.157, bf16[4096,512]{1,0:T(8,128)(2,1)} %bitcast.159, bf16[4096,256]{1,0:T(8,128)(2,1)S(1)} %bitcast.125, bf16[4096,256]{1,0:T(8,128)(2,1)S(1)} %bitcast.124), kind=kOutput, calls=%fused_computation.2 | convolution fusion | flops 4320133120 | bytes 14680064 | tf_op jit(solution)/shard_map/dot_general | solution.py:36
  19.7 0.0 copy-start.7
  19.7 0.2 fusion.16
  19.9 1.7 %subtract_convert_fusion.1 = (bf16[64,64,256]{2,1,0:T(8,128)(2,1)S(1)}, bf16[64,64,256]{2,1,0:T(8,128)(2,1)S(1)}) fusion(f32[64,256]{1,0:T(8,128)S(1)} %get-tuple-element.84, f32[64,256]{1,0:T(8,128)S(1)} %get-tuple-element.77, f32[64,256]{1,0:T(8,128)S(1)} %get-tuple-element.85, f32[64,256]{1,0:T(8,128)S(1)} %get-tuple-element.76), kind=kLoop, calls=%fused_computation.13 | loop fusion | flops 8388608 | bytes 4456448 | tf_op jit(solution)/shard_map/convert.19
  21.6 0.3 copy-done.7
  21.9 4.5 %fusion = f32[512,1024]{1,0:T(8,128)S(1)} fusion(bf16[4096,512]{1,0:T(8,128)(2,1)S(1)} %bitcast.158, bf16[4096,512]{1,0:T(8,128)(2,1)S(1)} %bitcast.160, bf16[4096,256]{1,0:T(8,128)(2,1)S(1)} %bitcast.127, bf16[4096,256]{1,0:T(8,128)(2,1)S(1)} %bitcast.126), kind=kOutput, calls=%fused_computation.1 | convolution fusion | flops 4320133120 | bytes 14680064 | tf_op jit(solution)/shard_map/dot_general | solution.py:36
  26.4 0.0 copy-start.1
  26.4 0.0 copy-start.4
  26.4 0.0 copy-start.3
  26.5 0.2 fusion.18
  26.6 0.1 maximum_maximum_fusion
  26.7 0.0 copy-start.2
  26.7 2.1 %copy.17 = bf16[2,2,256,512]{3,1,0,2:T(2,128)(2,1)} copy(bf16[2,2,256,512]{3,2,1,0:T(8,128)(2,1)S(1)} %maximum_maximum_fusion) | data formatting | bytes 2097152 | tf_op jit(solution)/shard_map/stack | solution.py:108
  28.8 5.2 %all-to-all-start = ((bf16[2,2,256,512]{3,1,0,2:T(2,128)(2,1)}), bf16[2,2,256,512]{3,1,0,2:T(2,128)(2,1)S(1)}, u32[]{:S(2)}, u32[]{:S(2)}) async-start(bf16[2,2,256,512]{3,1,0,2:T(2,128)(2,1)} %copy.17), calls=%async_computation | async-start | bytes 2097152 | tf_op jit(solution)/shard_map/all_to_all | solution.py:111
  34.0 0.2 reduce-scatter.2.cloned.1.call-start
  34.2 0.5 slice.258
  34.8 0.1 slice.213
  34.9 0.0 copy-done.1
  35.0 0.0 copy-done.4
  35.0 0.1 fusion.124
  35.0 0.6 slice_subtract_fusion.4
  35.7 0.0 copy-done.3
  35.7 0.7 cosine_multiply_fusion
  36.4 3.0 %subtract_convert_fusion = (bf16[64,64,256]{2,1,0:T(8,128)(2,1)S(1)}, bf16[64,64,256]{2,1,0:T(8,128)(2,1)}) fusion(f32[64,256]{1,0:T(8,128)S(1)} %get-tuple-element.80, f32[64,256]{1,0:T(8,128)S(1)} %get-tuple-element.69, f32[64,256]{1,0:T(8,128)S(1)} %get-tuple-element.81, f32[64,256]{1,0:T(8,128)S(1)} %get-tuple-element.68), kind=kLoop, calls=%fused_computation.11 | loop fusion | flops 8388608 | bytes 4456448 | tf_op jit(solution)/shard_map/convert.9
  39.4 0.0 copy-done.2
  39.4 0.1 copy.16
  39.5 1.3 %fusion.114 = (f32[2,4096]{1,0:T(2,128)S(1)}, f32[2,4096]{1,0:T(2,128)S(1)}, f32[2,4096]{1,0:T(2,128)S(1)}, f32[2,4096]{1,0:T(2,128)S(1)}) fusion(s32[4096]{0:T(1024)S(1)} %get-tuple-element.96, s32[4096]{0:T(1024)S(1)} %get-tuple-element.97, s32[2]{0:T(128)S(1)} %get-tuple-element.92, s32[2]{0:T(128)S(1)} %get-tuple-element.93), kind=kLoop, calls=%fused_computation.289 | loop fusion | flops 638976 | bytes 163856 | tf_op jit(solution)/shard_map/cos | solution.py:23
  40.8 8.6 %all-to-all-done = bf16[2,2,256,512]{3,1,0,2:T(2,128)(2,1)S(1)} async-done(((bf16[2,2,256,512]{3,1,0,2:T(2,128)(2,1)}), bf16[2,2,256,512]{3,1,0,2:T(2,128)(2,1)S(1)}, u32[]{:S(2)}, u32[]{:S(2)}) %all-to-all-start) | async-done | bytes 1048608 | tf_op jit(solution)/shard_map/all_to_all | solution.py:111
  49.4 0.6 copy.25
  50.0 0.0 copy-start
  50.0 0.3 slice_convert_fusion.3
  50.3 0.3 copy.20
  50.6 0.3 copy.21
  50.9 0.3 add_convert_fusion.4
  51.2 0.1 pad_maximum_fusion.3
  51.3 0.3 copy-done
  51.6 0.8 fusion.9
  52.4 0.3 copy.22
  52.7 0.3 copy.23
  53.0 0.3 add_convert_fusion.3
  53.3 0.1 pad_maximum_fusion.4
  53.4 0.8 fusion.8
  54.2 0.0 copy-start.5
  54.2 0.7 maximum_maximum_fusion.1
  54.9 0.0 reduce-scatter.2.cloned.1.call-update
  55.0 0.1 select_reduce_fusion
  55.1 19.4 %reduce-scatter.2.cloned.1.call-done = f32[1,32,512]{2,1,0:T(8,128)} async-done(((f32[4,32,512]{2,1,0:T(8,128)}), f32[1,32,512]{2,1,0:T(8,128)}) %reduce-scatter.2.cloned.1.call-update) | async-done | bytes 65552 | tf_op jit(solution)/shard_map/reduce_scatter | solution.py:120
  74.5 0.8 convert_element_type.187
  75.4 9.2 %all_gather.3 = bf16[1,256,512]{2,1,0:T(8,128)(2,1)S(1)} all-gather(bf16[1,32,512]{2,1,0:T(8,128)(2,1)S(1)} %convert_element_type.187), channel_id=1, replica_groups=mesh['facet'=4,'col'=8] {'col'}, dimensions={1}, use_global_device_ids=true | all-gather | bytes 294912 | tf_op jit(solution)/shard_map/all_gather | solution.py:134
  84.6 1.8 %convolution_bitcast_fusion = f32[1,512,512]{1,2,0:T(8,128)S(1)} fusion(bf16[1,256,512]{2,1,0:T(8,128)(2,1)S(1)} %all_gather.3, f32[512]{0:T(512)S(1)} %bitcast.149, s32[512]{0:T(512)S(1)} %get-tuple-element.65, f32[512]{0:T(512)S(1)} %bitcast.150, s32[512]{0:T(512)S(1)} %get-tuple-element.64, f32[512]{0:T(512)S(1)} %bitcast.151, ...), kind=kOutput, calls=%fused_computation.18 | convolution fusion | flops 137363456 | bytes 1343488 | tf_op jit(solution)/shard_map/svr,src->svc/dot_general | solution.py:131
  86.4 0.5 fusion.10
  86.9 0.0 copy-done.5
  86.9 0.7 bitcast_select_fusion
  (14 shorter events, 0.1 us)
Async XLA Ops:
  10.0 3.1 %copy-start.6 = (bf16[1,4096,512]{2,1,0:T(8,128)(2,1)S(1)}, bf16[1,4096,512]{2,1,0:T(8,128)(2,1)}, u32[]{:S(2)}) copy-start(bf16[1,4096,512]{2,1,0:T(8,128)(2,1)} %param.9) | copy-start | bytes 12582916
  19.7 2.2 %copy-start.7 = (bf16[1,4096,512]{2,1,0:T(8,128)(2,1)S(1)}, bf16[1,4096,512]{2,1,0:T(8,128)(2,1)}, u32[]{:S(2)}) copy-start(bf16[1,4096,512]{2,1,0:T(8,128)(2,1)} %param.8) | copy-start | bytes 12582916
  26.4 8.5 %copy-start.1 = (s32[2,1,4,128]{3,2,1,0:T(4,128)S(1)}, s32[2,1,4,128]{3,2,1,0:T(4,128)}, u32[]{:S(2)}) copy-start(s32[2,1,4,128]{3,2,1,0:T(4,128)} %param.14) | copy-start | bytes 12292
  26.4 8.5 %copy-start.4 = (s32[4]{0:T(128)S(1)}, s32[4]{0:T(128)}, u32[]{:S(2)}) copy-start(s32[4]{0:T(128)} %param.11) | copy-start | bytes 52
  26.4 9.2 %copy-start.3 = (s32[2,1,4,128]{3,2,1,0:T(4,128)S(1)}, s32[2,1,4,128]{3,2,1,0:T(4,128)}, u32[]{:S(2)}) copy-start(s32[2,1,4,128]{3,2,1,0:T(4,128)} %param.15) | copy-start | bytes 12292
  26.7 12.7 %copy-start.2 = (f32[16,8]{0,1:T(8,128)S(1)}, f32[16,8]{0,1:T(8,128)}, u32[]{:S(2)}) copy-start(f32[16,8]{0,1:T(8,128)} %param.12) | copy-start | bytes 1540
  28.8 20.6 %all-to-all-start = ((bf16[2,2,256,512]{3,1,0,2:T(2,128)(2,1)}), bf16[2,2,256,512]{3,1,0,2:T(2,128)(2,1)S(1)}, u32[]{:S(2)}, u32[]{:S(2)}) async-start(bf16[2,2,256,512]{3,1,0,2:T(2,128)(2,1)} %copy.17), calls=%async_computation | async-start | bytes 2097152 | tf_op jit(solution)/shard_map/all_to_all | solution.py:111
  34.0 40.5 %reduce-scatter.2.cloned.1.call-start = ((), (), s32[]{:S(2)}) async-start(), calls=%async_computation.2 | async-start | bytes 327680 | tf_op jit(solution)/shard_map/reduce_scatter | solution.py:120
  50.0 1.6 %copy-start = (bf16[64,64,256]{2,1,0:T(8,128)(2,1)S(1)}, bf16[64,64,256]{2,1,0:T(8,128)(2,1)}, u32[]{:S(2)}) copy-start(bf16[64,64,256]{2,1,0:T(8,128)(2,1)} %get-tuple-element.23) | copy-start | bytes 6291460
  54.2 32.8 %copy-start.5 = (s32[1,4]{1,0:T(1,128)S(1)}, s32[1,4]{1,0:T(1,128)}, u32[]{:S(2)}) copy-start(s32[1,4]{1,0:T(1,128)} %param.13) | copy-start | bytes 52
Sparse Core Ops, SparseCore 0:
  55.1 19.3 reduce-scatter.1

commit v2 on v0

v2 whole, which is shorter than its diff:
```python
import functools
import math

import jax
import jax.numpy as jnp
from jax import lax
from jax.experimental import pallas as pl
from jax.experimental.pallas import tpu as pltpu
from jax.sharding import PartitionSpec as P

N_IMG = 65536
MASK = N_IMG - 1
S = 256
SCOL = 2
LANES = 128
F32 = jnp.float32
BF16 = jnp.bfloat16


def unit(points):
    angles = points.astype(F32) * (2.0 * math.pi / N_IMG)
    return jnp.cos(angles), jnp.sin(angles)


def times(left, right):
    return (
        left[0] * right[0] - left[1] * right[1],
        left[0] * right[1] + left[1] * right[0],
    )


def iota(shape, dim):
    return lax.broadcasted_iota(jnp.int32, shape, dim)


def exclusive(left, right, count):
    total, bit = 0, 1
    while bit < count:
        total = total + ((left // bit) % 2 + (right // bit) % 2) % 2 * bit
        bit *= 2
    return total


def body(
    dims,
    coff_ref,
    soff_ref,
    kern_ref,
    count_ref,
    cell_ref,
    frac_ref,
    re_hbm,
    im_hbm,
    vre_ref,
    vim_ref,
    sky,
    table,
    prod,
    base,
    shift_tab,
    second,
    stacked,
    prod2,
    sendbuf,
    recv,
    zbuf,
    zrecv,
    grid,
    row_w,
    col_w,
    taps,
    sky_sem,
    send_sem,
    recv_sem,
    zsend_sem,
    zrecv_sem,
    gsend_sem,
    grecv_sem,
):
    n_f, n_c, pixels, cols, subs, owned, blocks, slots, groups, ksize, over = dims
    rows = S // groups
    rp = S // n_c
    dpg = n_c // groups
    per = subs // SCOL
    f = lax.axis_index("facet")
    c = lax.axis_index("col")

    loads = []
    for index, src in enumerate((re_hbm, im_hbm)):
        copy = pltpu.make_async_copy(
            src.at[0], sky.at[index], sky_sem.at[index]
        )
        copy.start()
        loads.append(copy)

    barrier = pltpu.get_barrier_semaphore()
    for step in range(1, n_c):
        pl.semaphore_signal(barrier, inc=1, device_id={"col": lax.rem(c + step, n_c)})
    for step in range(1, n_f):
        pl.semaphore_signal(barrier, inc=1, device_id={"facet": lax.rem(f + step, n_f)})

    jrow = iota((rows, LANES), 0)
    lane = iota((rows, LANES), 1)
    base[0], base[1] = unit(jrow * lane)
    base[2], base[3] = unit((jrow * LANES) & MASK)

    first_y = f * pixels + c * cols
    ycol = first_y + iota((subs, cols), 1)
    soff = soff_ref[...]
    points = ((soff * (ycol // 256)) & MASK) * 256 + soff * (ycol % 256)
    shift_tab[0], shift_tab[1] = unit(points & MASK)

    strip = 32
    kline = iota((strip, S), 1)
    mline = first_y + iota((strip, S), 0)
    points = ((mline // 256 * kline) & MASK) * 256 + (mline % 256) * kline
    now = unit(points & MASK)
    scale2 = 1.0 / math.sqrt(pixels * n_f)
    now = (now[0] * scale2, now[1] * scale2)
    stride = unit((strip * iota((8, S), 1)) & MASK)
    stride = (stride[0][0:1], stride[1][0:1])
    for part in range(cols // strip):
        here = slice(part * strip, (part + 1) * strip)
        second[here, :S] = now[0].astype(BF16)
        second[here, S:] = now[1].astype(BF16)
        now = times(now, stride)

    own_group = c // dpg
    scale1 = 1.0 / math.sqrt(pixels)

    def send(dest):
        return pltpu.make_async_remote_copy(
            src_ref=sendbuf.at[dest],
            dst_ref=recv.at[c],
            send_sem=send_sem.at[dest],
            recv_sem=recv_sem.at[c],
            device_id={"col": dest},
        )

    def fill_table(g):
        for q in range(SCOL):
            start = coff_ref[q] + g * rows
            ll = iota((8, LANES), 1)
            along = unit((start * ll) & MASK)
            along = (along[0][0:1] * scale1, along[1][0:1] * scale1)
            jump = unit((start * LANES + 0 * ll) & MASK)
            jump = (jump[0][0:1], jump[1][0:1])
            now = times((base[0], base[1]), along)
            jump = times((base[2], base[3]), jump)
            top = q * 2 * rows
            for part in range(pixels // LANES):
                lanes = slice(part * LANES, (part + 1) * LANES)
                table[top : top + rows, lanes] = now[0].astype(BF16)
                table[top + rows : top + 2 * rows, lanes] = now[1].astype(BF16)
                now = times(now, jump)

    def transform(g):
        for index in range(2):
            prod[:, index * cols : (index + 1) * cols] = jnp.dot(
                table[...], sky[index], preferred_element_type=F32
            )
        for q in range(SCOL):
            cos_rows = slice(q * 2 * rows, q * 2 * rows + rows)
            sin_rows = slice(q * 2 * rows + rows, (q + 1) * 2 * rows)
            band_re = prod[cos_rows, :cols] + prod[sin_rows, cols:]
            band_im = prod[cos_rows, cols:] - prod[sin_rows, :cols]
            band_re = band_re.astype(BF16).astype(F32)
            band_im = band_im.astype(BF16).astype(F32)
            for s in range(q * per, (q + 1) * per):
                sc = shift_tab[0, s : s + 1]
                sd = shift_tab[1, s : s + 1]
                at = s * 2 * rows
                stacked[at : at + rows] = (band_re * sc + band_im * sd).astype(BF16)
                stacked[at + rows : at + 2 * rows] = (band_im * sc - band_re * sd).astype(BF16)
        prod2[...] = jnp.dot(stacked[...], second[...], preferred_element_type=F32)
        for s in range(subs):
            for t in range(dpg):
                upper = slice(s * 2 * rows + t * rp, s * 2 * rows + (t + 1) * rp)
                lower = slice(upper.start + rows, upper.stop + rows)
                dest = g * dpg + t
                sendbuf[dest, s, :, :S] = (prod2[upper, :S] + prod2[lower, S:]).astype(BF16)
                sendbuf[dest, s, :, S:] = (prod2[lower, :S] - prod2[upper, S:]).astype(BF16)

    def group_at(step):
        return exclusive(own_group, groups - 1 - step, groups)

    fill_table(group_at(0))
    for copy in loads:
        copy.wait()
    transform(group_at(0))
    pl.semaphore_wait(barrier, n_c - 1 + n_f - 1)

    def one_group(step, carry):
        fill_table(group_at(step))
        for t in range(dpg):
            send(group_at(step - 1) * dpg + t).start()
        transform(group_at(step))
        return carry

    lax.fori_loop(1, groups, one_group, 0)

    total = owned * blocks
    frac = frac_ref[...]
    for tap in range(ksize):
        value = jnp.zeros(frac.shape, F32)
        for row in range(over):
            value = jnp.where(frac == row, kern_ref[row, tap], value)
        taps[tap] = value

    for t in range(dpg - 1):
        send(own_group * dpg + lax.rem(lax.rem(c, dpg) + 1 + t, dpg)).start()

    for b in range(total):
        lanes = slice(b * slots, (b + 1) * slots)
        away_row = iota((S, slots), 0) - cell_ref[b : b + 1]
        away_col = iota((S, slots), 0) - cell_ref[total + b : total + b + 1]
        row_val = jnp.zeros((S, slots), F32)
        col_val = jnp.zeros((S, slots), F32)
        for tap in range(ksize):
            row_val = jnp.where(away_row == tap, taps[tap, b : b + 1], row_val)
            col_val = jnp.where(away_col == tap, taps[tap, total + b : total + b + 1], col_val)
        row_w[:, lanes] = row_val.astype(BF16)
        col_w[:, lanes] = col_val

    for step in range(1, n_c):
        src = lax.rem(c + step, n_c)
        pltpu.make_async_remote_copy(
            src_ref=recv.at[src],
            dst_ref=recv.at[src],
            send_sem=send_sem.at[src],
            recv_sem=recv_sem.at[src],
            device_id={"col": src},
        ).wait_recv()
    for s in range(subs):
        acc = sendbuf[c, s].astype(F32)
        for step in range(1, n_c):
            acc = acc + recv[lax.rem(c + step, n_c), s].astype(F32)
        zbuf[s // owned, s % owned] = acc.astype(BF16)

    def zcopy(dest):
        return pltpu.make_async_remote_copy(
            src_ref=zbuf.at[dest],
            dst_ref=zrecv.at[f],
            send_sem=zsend_sem.at[dest],
            recv_sem=zrecv_sem.at[f],
            device_id={"facet": dest},
        )

    for step in range(1, n_f):
        zcopy(lax.rem(f + step, n_f)).start()
    for step in range(1, n_c):
        send(lax.rem(c + step, n_c)).wait_send()
    for step in range(1, n_f):
        src = lax.rem(f + step, n_f)
        pltpu.make_async_remote_copy(
            src_ref=zrecv.at[src],
            dst_ref=zrecv.at[src],
            send_sem=zsend_sem.at[src],
            recv_sem=zrecv_sem.at[src],
            device_id={"facet": src},
        ).wait_recv()
    acc = zbuf[f].astype(F32)
    for step in range(1, n_f):
        acc = acc + zrecv[lax.rem(f + step, n_f)].astype(F32)
    grid[c] = acc.astype(BF16)

    def gcopy(dest):
        return pltpu.make_async_remote_copy(
            src_ref=grid.at[c],
            dst_ref=grid.at[c],
            send_sem=gsend_sem.at[dest],
            recv_sem=grecv_sem.at[c],
            device_id={"col": dest},
        )

    for step in range(1, n_c):
        gcopy(lax.rem(c + step, n_c)).start()
    for step in range(1, n_f):
        zcopy(lax.rem(f + step, n_f)).wait_send()
    for step in range(1, n_c):
        src = lax.rem(c + step, n_c)
        pltpu.make_async_remote_copy(
            src_ref=grid.at[src],
            dst_ref=grid.at[src],
            send_sem=gsend_sem.at[src],
            recv_sem=grecv_sem.at[src],
            device_id={"col": src},
        ).wait_recv()
    for step in range(1, n_c):
        gcopy(lax.rem(c + step, n_c)).wait_send()

    for o in range(owned):
        cells = grid[:, o]
        if rp % 16 == 0:
            cells = cells.reshape(S, 2 * S)
        else:
            cells = cells.astype(F32).reshape(S, 2 * S).astype(BF16)
        for b in range(o * blocks, (o + 1) * blocks):
            lanes = slice(b * slots, (b + 1) * slots)
            summed = lax.dot_general(
                cells,
                row_w[:, lanes],
                (((0,), (0,)), ((), ())),
                preferred_element_type=F32,
            )
            weights = col_w[:, lanes]
            live = iota((1, slots), 1) < count_ref[b]
            vis_real = jnp.sum(summed[:S] * weights, axis=0, keepdims=True)
            vis_imag = jnp.sum(summed[S:] * weights, axis=0, keepdims=True)
            vre_ref[b : b + 1] = jnp.where(live, vis_real, 0.0)
            vim_ref[b : b + 1] = jnp.where(live, vis_imag, 0.0)


def local(sky_re, sky_im, col_offsets, sub_offsets, kernel, vis_count, cell_index, frac_index):
    n_f = lax.axis_size("facet")
    n_c = lax.axis_size("col")
    pixels, cols = sky_re.shape[1:]
    subs = sub_offsets.shape[0]
    owned, blocks = vis_count.shape
    slots = cell_index.shape[-1]
    over, ksize = kernel.shape
    groups = 4
    rows = S // groups
    rp = S // n_c
    total = owned * blocks
    dims = (n_f, n_c, pixels, cols, subs, owned, blocks, slots, groups, ksize, over)
    smem = pl.BlockSpec(memory_space=pltpu.SMEM)
    vmem = pl.BlockSpec(memory_space=pltpu.VMEM)
    anywhere = pl.BlockSpec(memory_space=pl.ANY)
    dma = pltpu.SemaphoreType.DMA
    out = jax.ShapeDtypeStruct((total, slots), F32)
    vis_real, vis_imag = pl.pallas_call(
        functools.partial(body, dims),
        out_shape=(out, out),
        in_specs=[smem, vmem, smem, smem, vmem, vmem, anywhere, anywhere],
        out_specs=(vmem, vmem),
        scratch_shapes=[
            pltpu.VMEM((2, pixels, cols), BF16),
            pltpu.VMEM((2 * SCOL * rows, pixels), BF16),
            pltpu.VMEM((2 * SCOL * rows, 2 * cols), F32),
            pltpu.VMEM((4, rows, LANES), F32),
            pltpu.VMEM((2, subs, cols), F32),
            pltpu.VMEM((cols, 2 * S), BF16),
            pltpu.VMEM((2 * subs * rows, cols), BF16),
            pltpu.VMEM((2 * subs * rows, 2 * S), F32),
            pltpu.VMEM((n_c, subs, rp, 2 * S), BF16),
            pltpu.VMEM((n_c, subs, rp, 2 * S), BF16),
            pltpu.VMEM((n_f, owned, rp, 2 * S), BF16),
            pltpu.VMEM((n_f, owned, rp, 2 * S), BF16),
            pltpu.VMEM((n_c, owned, rp, 2 * S), BF16),
            pltpu.VMEM((S, total * slots), BF16),
            pltpu.VMEM((S, total * slots), F32),
            pltpu.VMEM((ksize, 2 * total, slots), F32),
            dma((2,)),
            dma((n_c,)),
            dma((n_c,)),
            dma((n_f,)),
            dma((n_f,)),
            dma((n_c,)),
            dma((n_c,)),
        ],
        compiler_params=pltpu.CompilerParams(
            collective_id=0, has_side_effects=True, vmem_limit_bytes=56 << 20
        ),
    )(
        col_offsets,
        sub_offsets.reshape(subs, 1),
        kernel,
        vis_count.reshape(total),
        cell_index.reshape(2 * total, slots),
        frac_index.reshape(2 * total, slots),
        sky_re,
        sky_im,
    )
    shape = (owned, blocks, slots)
    return (vis_real.reshape(shape), vis_imag.reshape(shape))


def solution(mesh):
    placed = (
        P("facet", None, "col"),
        P("facet", None, "col"),
        P(),
        P(),
        P(),
        P("facet", "col"),
        P(None, "facet", "col", None),
        P(None, "facet", "col", None),
    )
    return jax.shard_map(
        local,
        mesh=mesh,
        in_specs=placed,
        out_specs=(P("facet", "col", None), P("facet", "col", None)),
        check_vma=False,
    )
```

time: 140 us -> 40.7 us (0.29)
  other arithmetic: 70.8 us -> 0 us
  Pallas kernels: 0 us -> 34.7 us
  waiting for transfers between devices: 21.7 us -> 0 us
  between operations: 14.4 us -> 0.64 us
  matrix products: 12.4 us -> 0 us
  blocking collectives: 9.25 us -> 0 us
  starting transfers between devices: 5.24 us -> 0 us
    another operation x7 -> x0, other arithmetic: 64.9 us -> none
    pallas_call x0 -> x1, Pallas kernels: none -> 34.7 us  [local(): pl.pallas_call(functools.partial(body, dims), out_shape=(out, out), in_sp...]
    reduce_scatter x1 -> x0, waiting for transfers between devices: 21.7 us -> none  [local(): lax.psum_scatter(partial_value, 'facet', scatter_dimension=0, tiled=True)]
    dot_general x5 -> x0, matrix products: 12.4 us -> none  [the longest x2 9.01 us: first_axis(): product = jnp.dot(table, facet_image, preferred_element_type=jnp.float32)]
    all_gather x1 -> x0, blocking collectives: 9.25 us -> none  [local(): lax.all_gather(grid_rows, 'col', axis=1, tiled=True)]
    all_to_all x1 -> x0, starting transfers between devices: 5.2 us -> none  [local(): lax.all_to_all(pieces, 'col', split_axis=2, concat_axis=3, tiled=True)]
    another operation x1 -> x0, local copies, waits for them, and re-layouts: 2.06 us -> none  [local(): jnp.stack([first_axis(facet_image, column_table(column), local_cols) for...]
    unnamed x21 -> x3, local copies, waits for them, and re-layouts: 1.78 us -> 3.82 us
  transfers between devices with their start and end apart: 2 -> 0, of which waited for: 1 -> 0; matrix products, arithmetic and copies ran while one was open for 18% -> 0% of each run, Pallas kernels for 0% -> 0%
where the time goes in v2:
time: 40.7 us; the launch traced here: 40.4 us
  Pallas kernels  34.7 us (85%)
  local copies, waits for them, and re-layouts  5.13 us (13%)
  between operations  0.64 us (2%)
    pallas_call x1, Pallas kernels, local(): pl.pallas_call(functools.partial(body, dims), out_shape=(out, out), in_sp...  34.7 us
    unnamed x3, local copies, waits for them, and re-layouts  3.82 us
    reshape x1, local copies, waits for them, and re-layouts, local(): sub_offsets.reshape(subs, 1)  1.31 us

profile of v2, /device:TPU:0, one launch (start us, length us, event | category | flops | bytes accessed | tf_op | source)
XLA Modules:
  0.0 40.4 jit_solution(10705917331013517809)
XLA Ops:
  0.6 1.3 %copy.10.soff_ref = s32[4,1]{1,0:T(4,128)} copy(s32[4,1]{0,1:T(1,128)} %bitcast.11) | data formatting | bytes 32 | tf_op jit(solution)/shard_map/reshape | solution.py:367
  1.9 1.3 %copy.11.kern_ref = f32[16,8]{1,0:T(8,128)} copy(f32[16,8]{0,1:T(8,128)} %param.12) | data formatting | bytes 1024 | tf_op args[4]
  3.3 34.7 %shard_map.95 = (f32[4,128]{1,0:T(4,128)}, f32[4,128]{1,0:T(4,128)}) custom-call(s32[2]{0:T(128)} %coff_ref.1, s32[4,1]{1,0:T(4,128)} %copy.10.soff_ref, f32[16,8]{1,0:T(8,128)} %copy.11.kern_ref, s32[4]{0:T(128)} %bitcast.10, s32[8,128]{1,0:T(8,128)} %bitcast.6, s32[8,128]{1,0:T(8,128)} %bitcast.7, bf16[1,4096,512]{2,1,0:T(8,128)(2,1)} %re_hbm.1, ...), custom_call_target="tpu_custom_call" | custom-call | tf_op jit(solution)/shard_map/pallas_call | solution.py:332
  38.0 1.2 %copy.14 = f32[1,4,128]{2,1,0:T(4,128)} copy(f32[1,4,128]{2,1,0:T(4,128)} %bitcast.9) | data formatting | bytes 4096
  39.2 1.2 %copy.15 = f32[1,4,128]{2,1,0:T(4,128)} copy(f32[1,4,128]{2,1,0:T(4,128)} %bitcast.8) | data formatting | bytes 4096

commit v3 on v2

--- a/solution.py
+++ b/solution.py
@@ -51,10 +51,10 @@
     frac_ref,
     re_hbm,
     im_hbm,
-    vre_ref,
-    vim_ref,
+    vis_ref,
     sky,
-    table,
+    table_a,
+    table_b,
     prod,
     base,
     shift_tab,
@@ -106,7 +106,10 @@
 
     first_y = f * pixels + c * cols
     ycol = first_y + iota((subs, cols), 1)
-    soff = soff_ref[...]
+    srow = iota((subs, cols), 0)
+    soff = jnp.zeros((subs, cols), jnp.int32)
+    for s in range(subs):
+        soff = jnp.where(srow == s, soff_ref[s], soff)
     points = ((soff * (ycol // 256)) & MASK) * 256 + soff * (ycol % 256)
     shift_tab[0], shift_tab[1] = unit(points & MASK)
 
@@ -137,8 +140,8 @@
             device_id={"col": dest},
         )
 
-    def fill_table(g):
-        for q in range(SCOL):
+    def fill_table(table, g, columns):
+        for q in columns:
             start = coff_ref[q] + g * rows
             ll = iota((8, LANES), 1)
             along = unit((start * ll) & MASK)
@@ -154,8 +157,9 @@
                 table[top + rows : top + 2 * rows, lanes] = now[1].astype(BF16)
                 now = times(now, jump)
 
-    def transform(g):
+    def transform(table, g, prepare):
         for index in range(2):
+            prepare(index)
             prod[:, index * cols : (index + 1) * cols] = jnp.dot(
                 table[...], sky[index], preferred_element_type=F32
             )
@@ -184,27 +188,31 @@
     def group_at(step):
         return exclusive(own_group, groups - 1 - step, groups)
 
-    fill_table(group_at(0))
-    for copy in loads:
-        copy.wait()
-    transform(group_at(0))
-    pl.semaphore_wait(barrier, n_c - 1 + n_f - 1)
-
-    def one_group(step, carry):
-        fill_table(group_at(step))
-        for t in range(dpg):
-            send(group_at(step - 1) * dpg + t).start()
-        transform(group_at(step))
-        return carry
-
-    lax.fori_loop(1, groups, one_group, 0)
+    tables = (table_a, table_b)
+    fill_table(tables[0], group_at(0), range(SCOL))
+    for step in range(groups):
+
+        def prepare(index, step=step):
+            if step == 0:
+                loads[index].wait()
+            if step + 1 < groups:
+                fill_table(
+                    tables[(step + 1) % 2], group_at(step + 1), range(index, SCOL, 2)
+                )
+            if index == 0 and step > 0:
+                for t in range(dpg):
+                    send(group_at(step - 1) * dpg + t).start()
+
+        transform(tables[step % 2], group_at(step), prepare)
+        if step == 0:
+            pl.semaphore_wait(barrier, n_c - 1 + n_f - 1)
 
     total = owned * blocks
     frac = frac_ref[...]
     for tap in range(ksize):
         value = jnp.zeros(frac.shape, F32)
         for row in range(over):
-            value = jnp.where(frac == row, kern_ref[row, tap], value)
+            value = jnp.where(frac == row, kern_ref[tap, row], value)
         taps[tap] = value
 
     for t in range(dpg - 1):
@@ -307,8 +315,8 @@
             live = iota((1, slots), 1) < count_ref[b]
             vis_real = jnp.sum(summed[:S] * weights, axis=0, keepdims=True)
             vis_imag = jnp.sum(summed[S:] * weights, axis=0, keepdims=True)
-            vre_ref[b : b + 1] = jnp.where(live, vis_real, 0.0)
-            vim_ref[b : b + 1] = jnp.where(live, vis_imag, 0.0)
+            vis_ref[b : b + 1] = jnp.where(live, vis_real, 0.0)
+            vis_ref[total + b : total + b + 1] = jnp.where(live, vis_imag, 0.0)
 
 
 def local(sky_re, sky_im, col_offsets, sub_offsets, kernel, vis_count, cell_index, frac_index):
@@ -328,14 +336,15 @@
     vmem = pl.BlockSpec(memory_space=pltpu.VMEM)
     anywhere = pl.BlockSpec(memory_space=pl.ANY)
     dma = pltpu.SemaphoreType.DMA
-    out = jax.ShapeDtypeStruct((total, slots), F32)
-    vis_real, vis_imag = pl.pallas_call(
+    out = jax.ShapeDtypeStruct((2 * total, slots), F32)
+    vis = pl.pallas_call(
         functools.partial(body, dims),
-        out_shape=(out, out),
-        in_specs=[smem, vmem, smem, smem, vmem, vmem, anywhere, anywhere],
-        out_specs=(vmem, vmem),
+        out_shape=out,
+        in_specs=[smem, smem, smem, smem, vmem, vmem, anywhere, anywhere],
+        out_specs=vmem,
         scratch_shapes=[
             pltpu.VMEM((2, pixels, cols), BF16),
+            pltpu.VMEM((2 * SCOL * rows, pixels), BF16),
             pltpu.VMEM((2 * SCOL * rows, pixels), BF16),
             pltpu.VMEM((2 * SCOL * rows, 2 * cols), F32),
             pltpu.VMEM((4, rows, LANES), F32),
@@ -364,16 +373,16 @@
         ),
     )(
         col_offsets,
-        sub_offsets.reshape(subs, 1),
-        kernel,
+        sub_offsets,
+        kernel.T,
         vis_count.reshape(total),
         cell_index.reshape(2 * total, slots),
         frac_index.reshape(2 * total, slots),
         sky_re,
         sky_im,
     )
-    shape = (owned, blocks, slots)
-    return (vis_real.reshape(shape), vis_imag.reshape(shape))
+    vis = vis.reshape(2, owned, blocks, slots)
+    return (vis[0], vis[1])
 
 
 def solution(mesh):

time: 40.7 us -> 35.7 us (0.88)
  local copies, waits for them, and re-layouts: 5.13 us -> 1.33 us
  Pallas kernels: 34.7 us -> 33.5 us
    unnamed x3 -> x0, local copies, waits for them, and re-layouts: 3.82 us -> none
    squeeze x0 -> x1, local copies, waits for them, and re-layouts: none -> 1.33 us  [local(): return (vis[0], vis[1])]
    reshape x1 -> x0, local copies, waits for them, and re-layouts: 1.31 us -> none  [local(): sub_offsets.reshape(subs, 1)]
    pallas_call x1, Pallas kernels: 34.7 us -> 33.5 us  [local(): pl.pallas_call(functools.partial(body, dims), out_shape=out, in_specs=[sm...]
where the time goes in v3:
time: 35.7 us; the launch traced here: 35.5 us
  Pallas kernels  33.5 us (94%)
  local copies, waits for them, and re-layouts  1.33 us (4%)
  between operations  0.64 us (2%)
    pallas_call x1, Pallas kernels, local(): pl.pallas_call(functools.partial(body, dims), out_shape=out, in_specs=[sm...  33.5 us
    squeeze x1, local copies, waits for them, and re-layouts, local(): return (vis[0], vis[1])  1.33 us

profile of v3, /device:TPU:0, one launch (start us, length us, event | category | flops | bytes accessed | tf_op | source)
XLA Modules:
  0.0 35.5 jit_solution(2555268494972908926)
XLA Ops:
  0.6 33.5 %shard_map.95 = f32[8,128]{1,0:T(8,128)} custom-call(s32[2]{0:T(128)} %coff_ref.1, s32[4]{0:T(128)} %soff_ref.1, f32[8,16]{1,0:T(8,128)} %bitcast.8, s32[4]{0:T(128)} %bitcast.11, s32[8,128]{1,0:T(8,128)} %bitcast.9, s32[8,128]{1,0:T(8,128)} %bitcast.10, bf16[1,4096,512]{2,1,0:T(8,128)(2,1)} %re_hbm.1, bf16[1,4096,512]{2,1,0:T(8,128)(2,1)} %im_hbm.1), custom_call_target="tpu_custom_call" | custom-call | tf_op jit(solution)/shard_map/pallas_call | solution.py:340
  34.1 1.3 %slice_bitcast_fusion = (f32[1,4,128]{2,1,0:T(4,128)}, f32[1,4,128]{2,1,0:T(4,128)}) fusion(f32[8,128]{1,0:T(8,128)} %shard_map.95), kind=kLoop, calls=%fused_computation | loop fusion | bytes 8192 | tf_op jit(solution)/shard_map/squeeze | solution.py:385
